TPU v7x, 32 devices: a whole 2x2x4 slice. The times are simulated.
32 devices in a mesh: dp: 2 (over x), row: 4 (over z), col: 4 (over y, core).
Axes of the slice: x: 2, y: 2, z: 4, core: 2. Of those that a mesh axis runs over, the one named last changes fastest.
Arguments:
- tokens: bfloat16 [16, 768, 1024], P(('dp', 'row'), 'col'), may hold values from -6 to 6
- memory: bfloat16 [16, 20, 768], P(('dp', 'row'), None, 'col'), may hold values from -6 to 6
- block_ids: int32 [16, 1024], P(('dp', 'row')), may hold values from 0 to 7, never falling along the last dimension, each value on 1 to 256 neighbouring positions
- valid: int32 [16], replicated, may hold values from 512 to 1024
- teacher: bfloat16 [16, 768, 1024], P(('dp', 'row'), 'col'), may hold values from -6 to 6
- w_qkv: bfloat16 [12, 147456], P('row', 'col'), may hold values from -0.21875 to 0.21875
- bias_qv: float32 [12, 128], P('row'), may hold values from -3 to 3
- w_out: bfloat16 [768, 768], P('row', 'col'), may hold values from -0.875 to 0.875
- bias_out: float32 [768], P('col'), may hold values from -2 to 2
- ln1_gain: float32 [768], P('col'), may hold values from 0.1 to 1.9
- ln1_bias: float32 [768], P('col'), may hold values from -2 to 2
- w_up: bfloat16 [768, 3072], P('col', 'row'), may hold values from -0.21875 to 0.21875
- bias_up: float32 [3072], P('row'), may hold values from -3 to 3
- w_down: bfloat16 [768, 3072], P('col', 'row'), may hold values from -0.109375 to 0.109375
- bias_down: float32 [768], P('col'), may hold values from -2 to 2
- ln2_gain: float32 [768], P('col'), may hold values from 0.1 to 1.9
- ln2_bias: float32 [768], P('col'), may hold values from -2 to 2
Outputs:
- layer_out: bfloat16 [16, 1044, 768], P(('dp', 'row'), None, 'col')
- grad_tokens: float32 [16, 1024, 768], P(('dp', 'row'), None, 'col')
- grad_memory: float32 [16, 20, 768], P(('dp', 'row'), None, 'col')
- grad_w_qkv: float32 [12, 147456], P('row', 'col')
- grad_bias_qv: float32 [12, 128], P('row')
- grad_w_out: float32 [768, 768], P('row', 'col')
- grad_bias_out: float32 [768], P('col')
- grad_ln1_gain: float32 [768], P('col')
- grad_ln1_bias: float32 [768], P('col')
- grad_w_up: float32 [768, 3072], P('col', 'row')
- grad_bias_up: float32 [3072], P('row')
- grad_w_down: float32 [768, 3072], P('col', 'row')
- grad_bias_down: float32 [768], P('col')
- grad_ln2_gain: float32 [768], P('col')
- grad_ln2_bias: float32 [768], P('col')
Inputs may be any that keep to these rules, and one draw needn't show every extreme that they name: `block_ids`: along each sequence the numbers never fall; each of the 8 numbers covers 1 to 256 consecutive tokens.
All inputs are finite; a program needn't handle non-finite values.
Results may differ from a plain program's by a relative error of at most 0.015.
Values may be sent and summed in bfloat16 or wider, within the bound.
A program may use at most 192 MiB of HBM per device.

v0:
```python
from functools import partial
import jax
import jax.numpy as jnp
from jax import lax
from jax.sharding import PartitionSpec as P

EPSILON = 1e-12
NEGATIVE = -1e30


def gather_feats(shard):
    return lax.all_gather(shard, "col", axis=1, tiled=True)


def back_gather(shard):
    return lax.all_gather(shard, "col", axis=1, tiled=True)


def forward_reduce(partial_rows):
    return lax.psum_scatter(
        partial_rows.astype(jnp.bfloat16), "col", scatter_dimension=1, tiled=True
    ).astype(jnp.float32)


def backward_reduce(partial_rows):
    return lax.psum_scatter(
        partial_rows.astype(jnp.bfloat16), "col", scatter_dimension=1, tiled=True
    ).astype(jnp.float32)


def against(piece_rows, matrix):
    return lax.dot_general(
        piece_rows, matrix, (((1,), (1,)), ((), ())), preferred_element_type=jnp.float32
    )


def column_total(piece_rows):
    unit_row = jnp.ones((1, piece_rows.shape[0]), jnp.bfloat16)
    return jnp.dot(unit_row, piece_rows, preferred_element_type=jnp.float32)[0]


def outer_sum(left_rows, right_rows):
    return lax.dot_general(
        left_rows, right_rows, (((0,), (0,)), ((), ())), preferred_element_type=jnp.float32
    )


def assemble(stacked, row_size, col_size):
    shape = stacked.shape
    grid = stacked.reshape((row_size, col_size) + shape[1:])
    moved = jnp.swapaxes(grid, 1, 2)
    return moved.reshape((row_size * shape[1], col_size * shape[2]) + shape[3:])


def norm_forward(summed, gain, shift, feat_total):
    sum_plain, sum_square = lax.psum(
        (jnp.sum(summed, axis=1), jnp.sum(summed * summed, axis=1)), "col"
    )
    average = sum_plain / feat_total
    inverse = lax.rsqrt(sum_square / feat_total - average * average + EPSILON)
    scaled = (summed - average[:, None]) * inverse[:, None]
    return (scaled * gain + shift, scaled, inverse)


def norm_backward(cotangent, scaled, inverse, gain, feat_total):
    weighted = cotangent * gain
    sum_plain, sum_cross = lax.psum(
        (jnp.sum(weighted, axis=1), jnp.sum(weighted * scaled, axis=1)), "col"
    )
    inner = weighted - sum_plain[:, None] / feat_total - scaled * (sum_cross[:, None] / feat_total)
    return (
        inverse[:, None] * inner,
        jnp.sum(cotangent * scaled, axis=0),
        jnp.sum(cotangent, axis=0),
    )


def visible_rows(token_ids, seq_rows):
    length = token_ids.shape[0]
    memory_rows = (seq_rows - length) // 2
    row_ids = jnp.concatenate(
        [
            jnp.full((memory_rows,), -1, jnp.int32),
            token_ids,
            jnp.full((memory_rows,), length, jnp.int32),
        ]
    )
    return row_ids[None, :] <= row_ids[:, None]


def masked_scores(queries, key_rows, token_ids):
    inv_root = queries.shape[-1] ** (-0.5)
    scores = (
        jnp.einsum("qhe,khe->hqk", queries, key_rows, preferred_element_type=jnp.float32) * inv_root
    )
    visible = visible_rows(token_ids, queries.shape[0])
    return jnp.where(visible[None], scores, NEGATIVE)


def attend(packed):
    queries, key_rows, values, token_ids = packed
    masked = masked_scores(queries, key_rows, token_ids)
    highest = jnp.max(masked, axis=-1, keepdims=True)
    exponent = jnp.exp(masked - highest)
    summed = jnp.sum(exponent, axis=-1, keepdims=True)
    attn_weights = (exponent / summed).astype(jnp.bfloat16)
    mixed_out = jnp.einsum("hqk,khe->qhe", attn_weights, values, preferred_element_type=jnp.float32)
    return (mixed_out.astype(jnp.bfloat16), (highest + jnp.log(summed))[..., 0])


def attend_back(packed):
    queries, key_rows, values, token_ids, log_totals, grad_mixed = packed
    inv_root = queries.shape[-1] ** (-0.5)
    masked = masked_scores(queries, key_rows, token_ids)
    probs_full = jnp.exp(masked - log_totals[..., None])
    attn_weights = probs_full.astype(jnp.bfloat16)
    grad_probs = jnp.einsum("qhe,khe->hqk", grad_mixed, values, preferred_element_type=jnp.float32)
    row_inner = jnp.sum(probs_full * grad_probs, axis=-1, keepdims=True)
    grad_scores = (probs_full * (grad_probs - row_inner)).astype(jnp.bfloat16)
    grad_queries = (
        jnp.einsum("hqk,khe->qhe", grad_scores, key_rows, preferred_element_type=jnp.float32)
        * inv_root
    )
    grad_keys = (
        jnp.einsum("hqk,qhe->khe", grad_scores, queries, preferred_element_type=jnp.float32)
        * inv_root
    )
    grad_values = jnp.einsum(
        "hqk,qhe->khe", attn_weights, grad_mixed, preferred_element_type=jnp.float32
    )
    return (
        grad_queries.astype(jnp.bfloat16),
        grad_keys.astype(jnp.bfloat16),
        grad_values.astype(jnp.bfloat16),
    )


def per_device(
    tokens,
    memory,
    block_ids,
    valid,
    teacher,
    w_qkv,
    bias_qv,
    w_out,
    bias_out,
    ln1_gain,
    ln1_bias,
    w_up,
    bias_up,
    w_down,
    bias_down,
    ln2_gain,
    ln2_bias,
):
    seq_count, feat_cols, length = tokens.shape
    memory_rows = memory.shape[1] // 2
    seq_rows = length + 2 * memory_rows
    row_count = seq_count * seq_rows
    row_size = lax.axis_size("row")
    col_size = lax.axis_size("col")
    row_place = lax.axis_index("row")
    col_place = lax.axis_index("col")
    head_rows = w_qkv.shape[0]
    head_size = bias_qv.shape[1] // 2
    feat_total = feat_cols * col_size
    head_local = head_rows * row_size // col_size
    unit_total = bias_up.shape[0] * row_size
    unit_local = unit_total // col_size
    qkv_blocks = w_qkv.reshape(head_rows, feat_cols, 3 * head_size)
    up_blocks = jnp.transpose(w_up)
    down_blocks = jnp.transpose(w_down)
    whole = (
        lax.all_gather(qkv_blocks[None], ("row", "col"), axis=0, tiled=True),
        lax.all_gather(w_out[None], ("row", "col"), axis=0, tiled=True),
        lax.all_gather(up_blocks[None], ("row", "col"), axis=0, tiled=True),
        lax.all_gather(down_blocks[None], ("row", "col"), axis=0, tiled=True),
    )
    full_qkv = assemble(whole[0], row_size, col_size)
    full_out = assemble(whole[1], row_size, col_size)
    full_up = assemble(whole[2], row_size, col_size)
    full_down = assemble(whole[3], row_size, col_size)
    qkv_heads = lax.dynamic_slice_in_dim(full_qkv, col_place * head_local, head_local, 0)
    out_rows = lax.dynamic_slice_in_dim(
        full_out, col_place * (head_local * head_size), head_local * head_size, 0
    )
    up_rows = lax.dynamic_slice_in_dim(full_up, col_place * unit_local, unit_local, 0)
    down_rows = lax.dynamic_slice_in_dim(full_down, col_place * unit_local, unit_local, 0)
    bias_heads_all, bias_units_all = (
        lax.all_gather(bias_qv, "row", axis=0, tiled=True),
        lax.all_gather(bias_up, "row", axis=0, tiled=True),
    )
    bias_heads = lax.dynamic_slice_in_dim(bias_heads_all, col_place * head_local, head_local, 0)
    bias_units = lax.dynamic_slice_in_dim(bias_units_all, col_place * unit_local, unit_local, 0)
    flat_qkv = jnp.transpose(qkv_heads, (1, 0, 2)).reshape(feat_total, head_local * 3 * head_size)
    token_rows = jnp.swapaxes(tokens, 1, 2)
    inputs = jnp.concatenate(
        [memory[:, :memory_rows], token_rows, memory[:, memory_rows:]], axis=1
    ).reshape(row_count, feat_cols)
    full_in = gather_feats(inputs)
    projected = jnp.dot(full_in, flat_qkv, preferred_element_type=jnp.float32).reshape(
        seq_count, seq_rows, head_local, 3 * head_size
    )
    queries = (projected[..., :head_size] + bias_heads[:, :head_size]).astype(jnp.bfloat16)
    key_rows = projected[..., head_size : 2 * head_size].astype(jnp.bfloat16)
    values = (projected[..., 2 * head_size :] + bias_heads[:, head_size:]).astype(jnp.bfloat16)
    mixed_out, log_totals = lax.map(attend, (queries, key_rows, values, block_ids))
    mixed_rows = mixed_out.reshape(row_count, head_local * head_size)
    attn_out = (
        forward_reduce(jnp.dot(mixed_rows, out_rows, preferred_element_type=jnp.float32)) + bias_out
    )
    norm_one, scaled_one, inverse_one = norm_forward(
        inputs.astype(jnp.float32) + attn_out, ln1_gain, ln1_bias, feat_total
    )
    norm_low = norm_one.astype(jnp.bfloat16)
    full_norm = gather_feats(norm_low)
    gate_pre = against(full_norm, up_rows) + bias_units
    hidden = jax.nn.gelu(gate_pre, approximate=False).astype(jnp.bfloat16)
    branch = (
        forward_reduce(jnp.dot(hidden, down_rows, preferred_element_type=jnp.float32)) + bias_down
    )
    output_rows, scaled_two, inverse_two = norm_forward(
        norm_one + branch, ln2_gain, ln2_bias, feat_total
    )
    output_seq = output_rows.reshape(seq_count, seq_rows, feat_cols)
    offset = lax.axis_index(("dp", "row")) * seq_count
    counts = lax.dynamic_slice_in_dim(valid, offset, seq_count, 0)
    loss_scale = valid.shape[0] * length / jnp.sum(valid).astype(jnp.float32)
    kept_rows = (jnp.arange(length, dtype=jnp.int32)[None, :] < counts[:, None])[..., None]
    mismatch = output_seq[:, memory_rows : memory_rows + length] - jnp.swapaxes(
        teacher, 1, 2
    ).astype(jnp.float32)
    grad_tok = jnp.where(kept_rows, loss_scale * mismatch, 0.0)
    grad_out = jnp.pad(grad_tok, ((0, 0), (memory_rows, memory_rows), (0, 0))).reshape(
        row_count, feat_cols
    )
    grad_two, gain_two, shift_two = norm_backward(
        grad_out, scaled_two, inverse_two, ln2_gain, feat_total
    )
    grad_branch = grad_two.astype(jnp.bfloat16)
    full_branch = back_gather(grad_branch)
    grad_down_rows = outer_sum(hidden, full_branch)
    grad_bias_down = column_total(grad_branch)
    grad_hidden = against(full_branch, down_rows)
    gelu_pull = jax.vjp(partial(jax.nn.gelu, approximate=False), gate_pre)[1]
    grad_gate = gelu_pull(grad_hidden)[0].astype(jnp.bfloat16)
    grad_up_rows = outer_sum(grad_gate, full_norm)
    grad_bias_units = column_total(grad_gate)
    grad_first = grad_two + backward_reduce(
        jnp.dot(grad_gate, up_rows, preferred_element_type=jnp.float32)
    )
    grad_one, gain_one, shift_one = norm_backward(
        grad_first, scaled_one, inverse_one, ln1_gain, feat_total
    )
    grad_attn = grad_one.astype(jnp.bfloat16)
    full_attn = back_gather(grad_attn)
    grad_out_rows = outer_sum(mixed_rows, full_attn)
    grad_bias_out = column_total(grad_attn)
    grad_mixed = against(full_attn, out_rows).astype(jnp.bfloat16)
    grad_mixed = grad_mixed.reshape(seq_count, seq_rows, head_local, head_size)
    grad_queries, grad_keys, grad_values = lax.map(
        attend_back, (queries, key_rows, values, block_ids, log_totals, grad_mixed)
    )
    grad_proj = jnp.concatenate([grad_queries, grad_keys, grad_values], axis=-1).reshape(
        row_count, head_local * 3 * head_size
    )
    grad_flat = outer_sum(full_in, grad_proj).reshape(feat_total, head_local, 3 * head_size)
    grad_heads = jnp.transpose(grad_flat, (1, 0, 2))
    proj_total = column_total(grad_proj).reshape(head_local, 3 * head_size)
    grad_bias_heads = jnp.concatenate(
        [proj_total[:, :head_size], proj_total[:, 2 * head_size :]], axis=1
    )
    grad_in = grad_one + backward_reduce(against(grad_proj, flat_qkv))
    relayed = (
        lax.all_to_all(
            grad_heads.astype(jnp.bfloat16), "col", split_axis=1, concat_axis=0, tiled=True
        ).astype(grad_heads.dtype),
        lax.all_to_all(
            grad_out_rows.astype(jnp.bfloat16), "col", split_axis=1, concat_axis=0, tiled=True
        ).astype(grad_out_rows.dtype),
        lax.all_to_all(
            grad_up_rows.astype(jnp.bfloat16), "col", split_axis=1, concat_axis=0, tiled=True
        ).astype(grad_up_rows.dtype),
        lax.all_to_all(
            grad_down_rows.astype(jnp.bfloat16), "col", split_axis=1, concat_axis=0, tiled=True
        ).astype(grad_down_rows.dtype),
    )
    grid_parts = (
        lax.psum_scatter(
            relayed[0].astype(jnp.bfloat16), "row", scatter_dimension=0, tiled=True
        ).astype(jnp.float32),
        lax.psum_scatter(
            relayed[1].astype(jnp.bfloat16), "row", scatter_dimension=0, tiled=True
        ).astype(jnp.float32),
        lax.psum_scatter(
            relayed[2].astype(jnp.bfloat16), "row", scatter_dimension=0, tiled=True
        ).astype(jnp.float32),
        lax.psum_scatter(
            relayed[3].astype(jnp.bfloat16), "row", scatter_dimension=0, tiled=True
        ).astype(jnp.float32),
    )
    weight_totals = (
        lax.psum(grid_parts[0].astype(jnp.bfloat16), "dp").astype(jnp.float32),
        lax.psum(grid_parts[1].astype(jnp.bfloat16), "dp").astype(jnp.float32),
        lax.psum(grid_parts[2].astype(jnp.bfloat16), "dp").astype(jnp.float32),
        lax.psum(grid_parts[3].astype(jnp.bfloat16), "dp").astype(jnp.float32),
    )
    grad_w_qkv = weight_totals[0].reshape(head_rows, feat_cols * 3 * head_size)
    grad_w_out = weight_totals[1]
    grad_w_up = jnp.transpose(weight_totals[2])
    grad_w_down = jnp.transpose(weight_totals[3])
    heads_pad = lax.dynamic_update_slice_in_dim(
        jnp.zeros((head_local * col_size, 2 * head_size), jnp.float32),
        grad_bias_heads,
        col_place * head_local,
        0,
    )
    units_pad = lax.dynamic_update_slice_in_dim(
        jnp.zeros((unit_total,), jnp.float32), grad_bias_units, col_place * unit_local, 0
    )
    feat_stack = jnp.stack(
        [gain_one, shift_one, gain_two, shift_two, grad_bias_out, grad_bias_down]
    )
    feat_pad = lax.dynamic_update_slice_in_dim(
        jnp.zeros((6, feat_total), jnp.float32), feat_stack, col_place * feat_cols, 1
    )
    small_totals = lax.psum((heads_pad, units_pad, feat_pad), ("dp", "row", "col"))
    grad_bias_qv = lax.dynamic_slice_in_dim(small_totals[0], row_place * head_rows, head_rows, 0)
    grad_bias_up = lax.dynamic_slice_in_dim(
        small_totals[1], row_place * bias_up.shape[0], bias_up.shape[0], 0
    )
    feat_totals = lax.dynamic_slice_in_dim(small_totals[2], col_place * feat_cols, feat_cols, 1)
    grad_seq = grad_in.reshape(seq_count, seq_rows, feat_cols)
    grad_tokens = grad_seq[:, memory_rows : memory_rows + length]
    grad_memory = jnp.concatenate(
        [grad_seq[:, :memory_rows], grad_seq[:, memory_rows + length :]], axis=1
    )
    return (
        output_seq.astype(jnp.bfloat16),
        grad_tokens,
        grad_memory,
        grad_w_qkv,
        grad_bias_qv,
        grad_w_out,
        feat_totals[4],
        feat_totals[0],
        feat_totals[1],
        grad_w_up,
        grad_bias_up,
        grad_w_down,
        feat_totals[5],
        feat_totals[2],
        feat_totals[3],
    )


def solution(mesh):
    in_specs = (
        P(("dp", "row"), "col", None),
        P(("dp", "row"), None, "col"),
        P(("dp", "row"), None),
        P(),
        P(("dp", "row"), "col", None),
        P("row", "col"),
        P("row", None),
        P("row", "col"),
        P("col"),
        P("col"),
        P("col"),
        P("col", "row"),
        P("row"),
        P("col", "row"),
        P("col"),
        P("col"),
        P("col"),
    )
    out_specs = (
        P(("dp", "row"), None, "col"),
        P(("dp", "row"), None, "col"),
        P(("dp", "row"), None, "col"),
        P("row", "col"),
        P("row", None),
        P("row", "col"),
        P("col"),
        P("col"),
        P("col"),
        P("col", "row"),
        P("row"),
        P("col", "row"),
        P("col"),
        P("col"),
        P("col"),
    )
    return jax.shard_map(
        per_device, mesh=mesh, in_specs=in_specs, out_specs=out_specs, check_vma=False
    )
```

profile of v0, /device:TPU:0, one launch (start us, length us, event | category | flops | bytes accessed | tf_op | source)
XLA Modules:
  0.0 976.6 jit_solution(16924794278916850676)
XLA Ops:
  14.5 13.6 %all-gather.3 = f32[4,3,128]{2,1,0:T(4,128)S(1)} all-gather(f32[1,3,128]{2,1,0:T(4,128)S(1)} %bitcast.266), channel_id=1, replica_groups=mesh['dp'=2,'row'=4,'col'=4] {'row'}, dimensions={0}, use_global_device_ids=true | all-gather | bytes 7680 | tf_op jit(solution)/shard_map/all_gather | solution.py:191
  28.2 24.4 %all-gather.24.cloned.1.call-done = bf16[3072,192]{1,0:T(8,128)(2,1)} async-done(((bf16[192,192]{1,0:T(8,128)(2,1)}), bf16[3072,192]{1,0:T(8,128)(2,1)}) %all-gather.24.cloned.1.call-update) | async-done | bytes 1179664 | tf_op jit(solution)/shard_map/all_gather | solution.py:176
  57.5 25.1 %all-gather.14.cloned.1.call-done = bf16[2088,768]{0,1:T(8,128)(2,1)} async-done(((bf16[2088,192]{0,1:T(8,128)(2,1)}), bf16[2088,768]{0,1:T(8,128)(2,1)}) %all-gather.14.cloned.1.call-update) | async-done | bytes 3207184 | tf_op jit(solution)/shard_map/all_gather | solution.py:12
  82.5 8.7 reshape.275
  91.2 47.3 %all-gather.16.cloned.1.call-done = bf16[16,3,192,192]{3,2,1,0:T(8,128)(2,1)} async-done(((bf16[1,3,192,192]{3,2,1,0:T(8,128)(2,1)}), bf16[16,3,192,192]{3,2,1,0:T(8,128)(2,1)}) %all-gather.16.cloned.1.call-update) | async-done | bytes 3538960 | tf_op jit(solution)/shard_map/all_gather | solution.py:175
  138.5 9.7 copy.108
  148.2 7.7 reshape.238
  155.9 4.6 fusion.60
  161.4 51.5 %while.26 = (s32[]{:T(128)}, bf16[2,1044,3,64]{1,3,2,0:T(8,128)(2,1)S(1)}, f32[2,3,1044]{2,1,0:T(4,128)}, bf16[2,1044,3,64]{1,3,2,0:T(8,128)(2,1)S(1)}, s32[2,10...) while((s32[]{:T(128)}, ...), condition=%wide.region_3.4_spmd, body=%wide.region_0.3_spmd.sunk | while | flops 864516608 | bytes 43690424 | solution.py:208
  163.9 8.0 fusion.151
  171.9 7.1 fusion.152
  179.0 7.8 fusion.153
  189.4 8.0 fusion.151
  197.4 7.1 fusion.152
  204.5 7.8 fusion.153
  218.0 4.0 convolution_convert_fusion.3
  223.5 36.4 %reduce-scatter.9.cloned.1.call-done = bf16[2088,192]{0,1:T(8,128)(2,1)} async-done(((bf16[2088,768]{0,1:T(8,128)(2,1)}), bf16[2088,192]{0,1:T(8,128)(2,1)}) %reduce-scatter.9.cloned.1.call-update) | async-done | bytes 801808 | tf_op jit(solution)/shard_map/reduce_scatter | solution.py:20
  261.6 10.3 %all-reduce.5 = (f32[2088]{0:T(1024)S(1)}, f32[2088]{0:T(1024)S(1)}) all-reduce(f32[2088]{0:T(1024)S(1)} %get-tuple-element.158, f32[2088]{0:T(1024)S(1)} %get-tuple-element.157), channel_id=1, replica_groups=mesh['dp'=2,'row'=4,'col'=4] {'col'}, use_global_device_ids=true, to_apply=%region_8.9 | all-reduce | flops 4176 | bytes 33408 | tf_op jit(solution)/shard_map/psum | solution.py:56
  274.6 13.3 %all-gather.4 = f32[4,1,768]{2,1,0:T(1,128)S(1)} all-gather(f32[1,1,768]{2,1,0:T(1,128)S(1)} %reshape.262), channel_id=1, replica_groups=mesh['dp'=2,'row'=4,'col'=4] {'row'}, dimensions={0}, use_global_device_ids=true | all-gather | bytes 15360 | tf_op jit(solution)/shard_map/all_gather | solution.py:192
  288.0 27.5 %all-gather.26.cloned.1.call-done = bf16[12288,192]{0,1:T(8,128)(2,1)} async-done(((bf16[768,192]{0,1:T(8,128)(2,1)}), bf16[12288,192]{0,1:T(8,128)(2,1)}) %all-gather.26.cloned.1.call-update) | async-done | bytes 4718608 | tf_op jit(solution)/shard_map/all_gather | solution.py:177
  315.5 8.2 reshape.243
  323.7 4.3 copy.111
  328.0 3.2 copy.143
  331.2 38.2 %all-gather.28.cloned.1.call-done = bf16[12288,192]{0,1:T(8,128)(2,1)} async-done(((bf16[768,192]{0,1:T(8,128)(2,1)}), bf16[12288,192]{0,1:T(8,128)(2,1)}) %all-gather.28.cloned.1.call-update) | async-done | bytes 4718608 | tf_op jit(solution)/shard_map/all_gather | solution.py:178
  369.4 8.3 reshape.245
  377.7 4.7 copy.112
  385.5 14.0 %all-gather.18.cloned.1.call-done = bf16[2088,768]{0,1:T(8,128)(2,1)} async-done(((bf16[2088,192]{0,1:T(8,128)(2,1)}), bf16[2088,768]{0,1:T(8,128)(2,1)}) %all-gather.18.cloned.1.call-update) | async-done | bytes 3207184 | tf_op jit(solution)/shard_map/all_gather | solution.py:12
  399.5 20.0 %multiply_convert_fusion.1 = (bf16[2088,768]{1,0:T(8,128)(2,1)S(1)}, f32[2088,768]{1,0:T(8,128)}, f32[2088,768]{1,0:T(8,128)}) fusion(f32[768]{0:T(1024)S(1)} %dynamic_slice.67, bf16[2088,768]{0,1:T(8,128)(2,1)} %all-gather.18.cloned.1.call-done, bf16[3072,768]{0,1:T(8,128)(2,1)} %bitcast.237, s32[]{:T(128)S(6)} %select_n.38), kind=kOutput, calls=%fused_computation.65 | convolution fusion | flops 2568941568 | bytes 20560900 | tf_op jit(solution)/shard_map/dot_general | solution.py:32
  421.2 5.9 convolution_convert_fusion.2
  429.2 37.2 %reduce-scatter.11.cloned.1.call-done = bf16[2088,192]{0,1:T(8,128)(2,1)} async-done(((bf16[2088,768]{0,1:T(8,128)(2,1)}), bf16[2088,192]{0,1:T(8,128)(2,1)}) %reduce-scatter.11.cloned.1.call-update) | async-done | bytes 801808 | tf_op jit(solution)/shard_map/reduce_scatter | solution.py:20
  468.7 10.6 %all-reduce.4 = (f32[2088]{0:T(1024)S(1)}, f32[2088]{0:T(1024)S(1)}) all-reduce(f32[2088]{0:T(1024)S(1)} %get-tuple-element.161, f32[2088]{0:T(1024)S(1)} %get-tuple-element.160), channel_id=1, replica_groups=mesh['dp'=2,'row'=4,'col'=4] {'col'}, use_global_device_ids=true, to_apply=%region_13.14 | all-reduce | flops 4176 | bytes 33408 | tf_op jit(solution)/shard_map/psum | solution.py:56
  480.9 3.5 reshape.247
  490.3 4.5 pad.4.clone
  494.8 3.2 reshape.248
  500.5 10.3 %all-reduce.3 = (f32[2088]{0:T(1024)S(1)}, f32[2088]{0:T(1024)S(1)}) all-reduce(f32[2088]{0:T(1024)S(1)} %get-tuple-element.155, f32[2088]{0:T(1024)S(1)} %reduce_sum.143), channel_id=1, replica_groups=mesh['dp'=2,'row'=4,'col'=4] {'col'}, use_global_device_ids=true, to_apply=%region_18.19 | all-reduce | flops 4176 | bytes 33408 | tf_op jit(solution)/shard_map/psum | solution.py:67
  514.1 29.9 %all-gather.20.cloned.1.call-done = bf16[2088,768]{0,1:T(8,128)(2,1)} async-done(((bf16[2088,192]{0,1:T(8,128)(2,1)}), bf16[2088,768]{0,1:T(8,128)(2,1)}) %all-gather.20.cloned.1.call-update) | async-done | bytes 3207184 | tf_op jit(solution)/shard_map/all_gather | solution.py:16
  544.0 10.5 %add_convert_fusion = bf16[2088,768]{1,0:T(8,128)(2,1)S(1)} fusion(f32[2088,768]{1,0:T(8,128)} %get-tuple-element.216, f32[2088,768]{1,0:T(8,128)} %get-tuple-element.241, bf16[2088,768]{0,1:T(8,128)(2,1)} %all-gather.20.cloned.1.call-done, bf16[3072,768]{0,1:T(8,128)(2,1)} %bitcast.240, s32[]{:T(128)S(6)} %select_n.38), kind=kOutput, calls=%fused_computation.64 | convolution fusion | flops 2485555200 | bytes 20557828 | tf_op jit(solution)/shard_map/dot_general | solution.py:32
  556.2 6.0 convolution_convert_fusion.1
  562.3 39.2 %reduce-scatter.13.cloned.1.call-done = bf16[2088,192]{0,1:T(8,128)(2,1)} async-done(((bf16[2088,768]{0,1:T(8,128)(2,1)}), bf16[2088,192]{0,1:T(8,128)(2,1)}) %reduce-scatter.13.cloned.1.call-update) | async-done | bytes 801808 | tf_op jit(solution)/shard_map/reduce_scatter | solution.py:26
  601.5 5.0 multiply_reduce_fusion.3
  606.5 10.3 %all-reduce.2 = (f32[2088]{0:T(1024)S(1)}, f32[2088]{0:T(1024)S(1)}) all-reduce(f32[2088]{0:T(1024)S(1)} %get-tuple-element.153, f32[2088]{0:T(1024)S(1)} %get-tuple-element.156), channel_id=1, replica_groups=mesh['dp'=2,'row'=4,'col'=4] {'col'}, use_global_device_ids=true, to_apply=%region_23.24 | all-reduce | flops 4176 | bytes 33408 | tf_op jit(solution)/shard_map/psum | solution.py:67
  620.3 30.1 %all-gather.22.cloned.1.call-done = bf16[2088,768]{0,1:T(8,128)(2,1)} async-done(((bf16[2088,192]{0,1:T(8,128)(2,1)}), bf16[2088,768]{0,1:T(8,128)(2,1)}) %all-gather.22.cloned.1.call-update) | async-done | bytes 3207184 | tf_op jit(solution)/shard_map/all_gather | solution.py:16
  650.4 3.7 convolution_convert_fusion.4
  660.9 68.2 %while.27 = (s32[]{:T(128)}, bf16[2,1044,3,64]{1,3,2,0:T(8,128)(2,1)}, bf16[2,1044,3,64]{1,3,2,0:T(8,128)(2,1)}, bf16[2,1044,3,64]{1,3,2,0:T(8,128)(2,1)}, bf16[...) while((s32[]{:T(128)}, ...), condition=%wide.region_26.27_spmd, body=%wide.region_24.26_spmd.sunk | while | flops 2124194560 | bytes 151329200 | solution.py:262
  661.8 3.4 fusion.162
  665.2 8.2 multiply_reduce_fusion.10
  673.5 8.6 multiply_convert_fusion.3
  682.1 8.3 fusion.165
  695.8 3.4 fusion.162
  699.2 8.2 multiply_reduce_fusion.10
  707.5 8.6 multiply_convert_fusion.3
  716.0 8.3 fusion.165
  736.8 5.0 fusion.72
  742.7 22.5 %all_to_all.75 = bf16[3,768,192]{2,0,1:T(4,128)(2,1)S(1)} all-to-all(bf16[3,768,192]{2,0,1:T(4,128)(2,1)S(1)} %copy.121), channel_id=1, replica_groups=mesh['dp'=2,'row'=4,'col'=4] {'col'}, dimensions={1} | all-to-all | bytes 1769472 | tf_op jit(solution)/shard_map/all_to_all | solution.py:276
  767.6 4.8 convolution_convert_fusion.5
  772.4 18.5 %all_to_all.76 = bf16[768,4,192]{0,2,1:T(8,128)(2,1)S(1)} all-to-all(bf16[768,4,192]{0,2,1:T(8,128)(2,1)S(1)} %bitcast.250), channel_id=1, replica_groups=mesh['dp'=2,'row'=4,'col'=4] {'col'}, dimensions={1} | all-to-all | bytes 2359296 | tf_op jit(solution)/shard_map/all_to_all | solution.py:285
  792.2 4.9 convolution_convert_fusion.6
  797.1 18.4 %all_to_all.77 = bf16[768,4,192]{0,2,1:T(8,128)(2,1)S(1)} all-to-all(bf16[768,4,192]{0,2,1:T(8,128)(2,1)S(1)} %bitcast.251), channel_id=1, replica_groups=mesh['dp'=2,'row'=4,'col'=4] {'col'}, dimensions={1} | all-to-all | bytes 2359296 | tf_op jit(solution)/shard_map/all_to_all | solution.py:282
  820.7 10.6 %all_to_all.78 = bf16[192,4,192]{2,0,1:T(8,128)(2,1)} all-to-all(bf16[192,4,192]{2,0,1:T(8,128)(2,1)S(1)} %copy.124), channel_id=1, replica_groups=mesh['dp'=2,'row'=4,'col'=4] {'col'}, dimensions={1} | all-to-all | bytes 589824 | tf_op jit(solution)/shard_map/all_to_all | solution.py:279
  833.5 22.8 %reduce-scatter.21.cloned.1.call-done = bf16[768,192]{0,1:T(8,128)(2,1)} async-done(((bf16[3072,192]{0,1:T(8,128)(2,1)}), bf16[768,192]{0,1:T(8,128)(2,1)}) %reduce-scatter.21.cloned.1.call-update) | async-done | bytes 294928 | tf_op jit(solution)/shard_map/reduce_scatter | solution.py:296
  856.3 21.5 %reduce-scatter.19.cloned.1.call-done = bf16[192,192]{1,0:T(8,128)(2,1)} async-done(((bf16[768,192]{1,0:T(8,128)(2,1)}), bf16[192,192]{1,0:T(8,128)(2,1)}) %reduce-scatter.19.cloned.1.call-update) | async-done | bytes 73744 | tf_op jit(solution)/shard_map/reduce_scatter | solution.py:293
  877.9 5.8 convolution_convert_fusion
  893.4 39.6 %all-reduce.1 = (f32[12,128]{1,0:T(8,128)S(1)}, f32[6,768]{1,0:T(8,128)S(1)}, f32[3072]{0:T(1024)S(1)}) all-reduce(f32[12,128]{1,0:T(8,128)S(1)} %dynamic_update_slice.26, f32[6,768]{1,0:T(8,128)S(1)} %dynamic_update_slice.27, f32[3072]{0:T(1024)S(1)} %dynamic_update_slice.28), channel_id=1, replica_groups=mesh['dp'=2,'row'=4,'col'=4] {'dp','row','col'}, use_global_device_ids=true, to_apply=%region_30.31 | all-reduce | flops 9216 | bytes 73728 | tf_op jit(solution)/shard_map/psum | solution.py:328
  942.1 17.5 %reduce-scatter.15.cloned.1.call-done = bf16[2088,192]{0,1:T(8,128)(2,1)} async-done(((bf16[2088,768]{0,1:T(8,128)(2,1)}), bf16[2088,192]{0,1:T(8,128)(2,1)}) %reduce-scatter.15.cloned.1.call-update) | async-done | bytes 801808 | tf_op jit(solution)/shard_map/reduce_scatter | solution.py:26
  (285 shorter events, 122.0 us)
Async XLA Ops:
  7.2 45.4 %all-gather.24.cloned.1.call-start = ((), (), s32[]{:S(2)}) async-start(), calls=%async_computation.25 | async-start | bytes 1671168 | tf_op jit(solution)/shard_map/all_gather | solution.py:176
  7.9 74.6 %all-gather.14.cloned.1.call-start = ((), (), s32[]{:S(2)}) async-start(), calls=%async_computation.12 | async-start | bytes 4177920 | tf_op jit(solution)/shard_map/all_gather | solution.py:12
  8.7 4.6 copy-start.30
  9.0 5.5 copy-start.51
  13.3 125.2 %all-gather.16.cloned.1.call-start = ((), (), s32[]{:S(2)}) async-start(), calls=%async_computation.13 | async-start | bytes 5013504 | tf_op jit(solution)/shard_map/all_gather | solution.py:175
  14.4 245.5 %reduce-scatter.9.cloned.1.call-start = ((), (), s32[]{:S(2)}) async-start(), calls=%async_computation.14 | async-start | bytes 4177920 | tf_op jit(solution)/shard_map/reduce_scatter | solution.py:20
  155.9 4.7 copy-start.24
  179.0 7.8 copy-start.31
  179.0 8.4 copy-start.35
  204.5 7.8 copy-start.31
  204.5 8.4 copy-start.35
  212.9 5.1 copy-start.3
  212.9 9.1 copy-start.5
  222.0 37.9 %copy-start.1 = (bf16[2088,192]{0,1:T(8,128)(2,1)S(1)}, bf16[2088,192]{0,1:T(8,128)(2,1)}, u32[]{:S(2)}) copy-start(bf16[2088,192]{0,1:T(8,128)(2,1)} %reshape.236) | copy-start | bytes 2405380
  222.0 37.9 %copy-start.40 = (f32[192]{0:T(256)S(1)}, f32[192]{0:T(256)}, u32[]{:S(2)}) copy-start(f32[192]{0:T(256)} %param.29) | copy-start | bytes 2308
  222.1 49.8 %copy-start.43 = (f32[192]{0:T(256)S(1)}, f32[192]{0:T(256)}, u32[]{:S(2)}) copy-start(f32[192]{0:T(256)} %param.30) | copy-start | bytes 2308
  222.1 49.8 %copy-start.45 = (f32[192]{0:T(256)S(1)}, f32[192]{0:T(256)}, u32[]{:S(2)}) copy-start(f32[192]{0:T(256)} %param.31) | copy-start | bytes 2308
  222.1 52.5 %copy-start.49 = (f32[768]{0:T(1024)S(1)}, f32[768]{0:T(1024)}, u32[]{:S(2)}) copy-start(f32[768]{0:T(1024)} %param.33) | copy-start | bytes 9220
  222.1 93.4 %all-gather.26.cloned.1.call-start = ((), (), s32[]{:S(2)}) async-start(), calls=%async_computation.26 | async-start | bytes 5013504 | tf_op jit(solution)/shard_map/all_gather | solution.py:177
  222.7 146.7 %all-gather.28.cloned.1.call-start = ((), (), s32[]{:S(2)}) async-start(), calls=%async_computation.27 | async-start | bytes 5013504 | tf_op jit(solution)/shard_map/all_gather | solution.py:178
  223.3 176.3 %all-gather.18.cloned.1.call-start = ((), (), s32[]{:S(2)}) async-start(), calls=%async_computation.15 | async-start | bytes 4177920 | tf_op jit(solution)/shard_map/all_gather | solution.py:12
  271.9 345.0 %copy-start.26 = (f32[2088]{0:T(1024)}, f32[2088]{0:T(1024)S(1)}, u32[]{:S(2)}) copy-start(f32[2088]{0:T(1024)S(1)} %get-tuple-element.235) | copy-start | bytes 25060
  271.9 345.0 %copy-start.28 = (f32[2088]{0:T(1024)}, f32[2088]{0:T(1024)S(1)}, u32[]{:S(2)}) copy-start(f32[2088]{0:T(1024)S(1)} %get-tuple-element.236) | copy-start | bytes 25060
  274.6 191.9 %reduce-scatter.11.cloned.1.call-start = ((), (), s32[]{:S(2)}) async-start(), calls=%async_computation.16 | async-start | bytes 4177920 | tf_op jit(solution)/shard_map/reduce_scatter | solution.py:20
  427.1 39.3 %copy-start.8 = (bf16[2088,192]{0,1:T(8,128)(2,1)S(1)}, bf16[2088,192]{0,1:T(8,128)(2,1)}, u32[]{:S(2)}) copy-start(bf16[2088,192]{0,1:T(8,128)(2,1)} %reduce-scatter.9.cloned.1.call-done) | copy-start | bytes 2405380
  427.1 39.3 %copy-start.52 = (f32[192]{0:T(256)S(1)}, f32[192]{0:T(256)}, u32[]{:S(2)}) copy-start(f32[192]{0:T(256)} %param.35) | copy-start | bytes 2308
  427.1 52.2 %copy-start.42 = (f32[192]{0:T(256)S(1)}, f32[192]{0:T(256)}, u32[]{:S(2)}) copy-start(f32[192]{0:T(256)} %param.36) | copy-start | bytes 2308
  427.1 52.2 %copy-start.53 = (f32[192]{0:T(256)S(1)}, f32[192]{0:T(256)}, u32[]{:S(2)}) copy-start(f32[192]{0:T(256)} %param.37) | copy-start | bytes 2308
  427.2 116.8 %all-gather.20.cloned.1.call-start = ((), (), s32[]{:S(2)}) async-start(), calls=%async_computation.17 | async-start | bytes 4177920 | tf_op jit(solution)/shard_map/all_gather | solution.py:16
  513.6 87.9 %reduce-scatter.13.cloned.1.call-start = ((), (), s32[]{:S(2)}) async-start(), calls=%async_computation.18 | async-start | bytes 4177920 | tf_op jit(solution)/shard_map/reduce_scatter | solution.py:26
  562.2 88.1 %all-gather.22.cloned.1.call-start = ((), (), s32[]{:S(2)}) async-start(), calls=%async_computation.19 | async-start | bytes 4177920 | tf_op jit(solution)/shard_map/all_gather | solution.py:16
  616.8 37.3 %copy-start.36 = (f32[2088]{0:T(1024)}, f32[2088]{0:T(1024)S(1)}, u32[]{:S(2)}) copy-start(f32[2088]{0:T(1024)S(1)} %broadcast_multiply_fusion) | copy-start | bytes 25060
  616.8 37.3 %copy-start.38 = (f32[2088]{0:T(1024)}, f32[2088]{0:T(1024)S(1)}, u32[]{:S(2)}) copy-start(f32[2088]{0:T(1024)S(1)} %broadcast_multiply_fusion.1) | copy-start | bytes 25060
  620.0 211.4 %reduce-scatter.17.cloned.1.call-start = ((), (), s32[]{:S(2)}) async-start(), calls=%async_computation.21 | async-start | bytes 1474560 | tf_op jit(solution)/shard_map/reduce_scatter | solution.py:290
  654.1 6.8 copy-start.4
  654.1 6.8 copy-start.6
  654.1 6.8 copy-start.33
  673.5 8.6 copy-start.7
  682.0 8.3 copy-start
  682.0 8.3 copy-start.17
  707.5 8.6 copy-start.7
  716.0 8.3 copy-start
  716.0 8.3 copy-start.17
  766.5 67.0 %reduce-scatter.23.cloned.1.call-start = ((), (), s32[]{:S(2)}) async-start(), calls=%async_computation.24 | async-start | bytes 1474560 | tf_op jit(solution)/shard_map/reduce_scatter | solution.py:299
  772.4 19.8 %copy-start.22 = (bf16[2088,768]{1,0:T(8,128)(2,1)S(1)}, bf16[2088,768]{1,0:T(8,128)(2,1)}, u32[]{:S(2)}) copy-start(bf16[2088,768]{1,0:T(8,128)(2,1)} %copy-done.21) | copy-start | bytes 9621508
  792.2 64.2 %reduce-scatter.21.cloned.1.call-start = ((), (), s32[]{:S(2)}) async-start(), calls=%async_computation.23 | async-start | bytes 1474560 | tf_op jit(solution)/shard_map/reduce_scatter | solution.py:296
  797.1 20.1 %copy-start.13 = (bf16[2088,192]{0,1:T(8,128)(2,1)S(1)}, bf16[2088,192]{0,1:T(8,128)(2,1)}, u32[]{:S(2)}) copy-start(bf16[2088,192]{0,1:T(8,128)(2,1)} %copy-done.12) | copy-start | bytes 2405380
  816.7 61.1 %reduce-scatter.19.cloned.1.call-start = ((), (), s32[]{:S(2)}) async-start(), calls=%async_computation.22 | async-start | bytes 491520 | tf_op jit(solution)/shard_map/reduce_scatter | solution.py:293
  820.3 57.6 %copy-start.15 = (bf16[2088,576]{0,1:T(8,128)(2,1)S(1)}, bf16[2088,576]{0,1:T(8,128)(2,1)}, u32[]{:S(2)}) copy-start(bf16[2088,576]{0,1:T(8,128)(2,1)} %reshape.250) | copy-start | bytes 7216132
  831.4 103.6 %all-reduce.9.cloned.1.call-start = ((), (), s32[]{:S(2)}) async-start(), calls=%async_computation.28 | async-start | bytes 1966080 | tf_op jit(solution)/shard_map/psum | solution.py:304
  877.9 81.7 %reduce-scatter.15.cloned.1.call-start = ((), (), s32[]{:S(2)}) async-start(), calls=%async_computation.20 | async-start | bytes 4177920 | tf_op jit(solution)/shard_map/reduce_scatter | solution.py:26
  885.5 4.8 copy-start.46
  885.5 4.8 copy-start.47
  885.5 4.9 copy-start.48
  885.5 4.9 copy-start.50
  888.6 70.9 %copy-start.2 = (bf16[2088,192]{0,1:T(8,128)(2,1)S(1)}, bf16[2088,192]{0,1:T(8,128)(2,1)}, u32[]{:S(2)}) copy-start(bf16[2088,192]{0,1:T(8,128)(2,1)} %reshape.236) | copy-start | bytes 2405380
  888.6 70.9 %copy-start.9 = (bf16[2088,192]{0,1:T(8,128)(2,1)S(1)}, bf16[2088,192]{0,1:T(8,128)(2,1)}, u32[]{:S(2)}) copy-start(bf16[2088,192]{0,1:T(8,128)(2,1)} %reduce-scatter.9.cloned.1.call-done) | copy-start | bytes 2405380
  888.6 70.9 %copy-start.11 = (f32[2088,192]{0,1:T(8,128)S(1)}, f32[2088,192]{0,1:T(8,128)}, u32[]{:S(2)}) copy-start(f32[2088,192]{0,1:T(8,128)} %get-tuple-element.213) | copy-start | bytes 4810756
  888.6 70.9 %copy-start.27 = (f32[2088]{0:T(1024)S(1)}, f32[2088]{0:T(1024)}, u32[]{:S(2)}) copy-start(f32[2088]{0:T(1024)} %copy-done.26) | copy-start | bytes 25060
  888.6 70.9 %copy-start.29 = (f32[2088]{0:T(1024)S(1)}, f32[2088]{0:T(1024)}, u32[]{:S(2)}) copy-start(f32[2088]{0:T(1024)} %copy-done.28) | copy-start | bytes 25060
  888.6 70.9 %copy-start.37 = (f32[2088]{0:T(1024)S(1)}, f32[2088]{0:T(1024)}, u32[]{:S(2)}) copy-start(f32[2088]{0:T(1024)} %copy-done.36) | copy-start | bytes 25060
  888.7 70.9 %copy-start.39 = (f32[2088]{0:T(1024)S(1)}, f32[2088]{0:T(1024)}, u32[]{:S(2)}) copy-start(f32[2088]{0:T(1024)} %copy-done.38) | copy-start | bytes 25060
  888.7 70.9 %copy-start.41 = (f32[192]{0:T(256)S(1)}, f32[192]{0:T(256)}, u32[]{:S(2)}) copy-start(f32[192]{0:T(256)} %param.29) | copy-start | bytes 2308
  888.7 70.9 %copy-start.44 = (f32[192]{0:T(256)S(1)}, f32[192]{0:T(256)}, u32[]{:S(2)}) copy-start(f32[192]{0:T(256)} %param.30) | copy-start | bytes 2308
  (19 other events, 30.9 us)
Sparse Core Ops, SparseCore 0:
  10.3 42.2 all-gather.23
  54.2 28.3 all-gather.13
  85.4 53.1 all-gather.15
  222.2 37.6 reduce-scatter.8
  262.0 53.4 all-gather.25
  317.6 51.7 all-gather.27
  371.5 27.9 all-gather.17
  427.3 39.0 reduce-scatter.10
  513.7 30.2 all-gather.19
  562.3 39.1 reduce-scatter.12
  620.2 30.1 all-gather.21
  766.6 29.3 reduce-scatter.16
  798.3 27.9 reduce-scatter.22
  828.4 27.9 reduce-scatter.20
  858.5 19.3 reduce-scatter.18
  880.8 37.2 all-reduce.8
  920.5 39.0 reduce-scatter.14
where the time goes:
time: 987 us; the launch traced here: 977 us
  waiting for transfers between devices  413 us (42%)
  blocking collectives  178 us (18%)
  matrix products  162 us (16%)
  local copies, waits for them, and re-layouts  134 us (14%)
  other arithmetic  71.6 us (7%)
  between operations  15.7 us (2%)
    reduce_scatter x2, waiting for transfers between devices, forward_reduce(): lax.psum_scatter(partial_rows.astype(jnp.bfloat16), 'col', scatter_dimens...  73.6 us
    all_gather x2, waiting for transfers between devices, back_gather(): return lax.all_gather(shard, 'col', axis=1, tiled=True)  60 us
    reduce_scatter x2, waiting for transfers between devices, backward_reduce(): lax.psum_scatter(partial_rows.astype(jnp.bfloat16), 'col', scatter_dimens...  56.7 us
    all_gather x1, waiting for transfers between devices, per_device(): lax.all_gather(qkv_blocks[None], ('row', 'col'), axis=0, tiled=True)  47.3 us
    dot_general x4, matrix products, against(): lax.dot_general(piece_rows, matrix, (((1,), (1,)), ((), ())), preferred_e...  40 us
    psum x1, blocking collectives, per_device(): lax.psum((heads_pad, units_pad, feat_pad), ('dp', 'row', 'col'))  39.6 us
    all_gather x2, waiting for transfers between devices, gather_feats(): return lax.all_gather(shard, 'col', axis=1, tiled=True)  39.1 us
    all_gather x1, waiting for transfers between devices, per_device(): lax.all_gather(down_blocks[None], ('row', 'col'), axis=0, tiled=True)  38.2 us
  transfers between devices with their start and end apart: 17, of which 14 were waited for; matrix products, arithmetic and copies ran while one was open for 10% of the time, Pallas kernels for 0%

commit v1 on v0

--- a/solution.py
+++ b/solution.py
@@ -1,11 +1,31 @@
+import functools
 from functools import partial
 import jax
 import jax.numpy as jnp
 from jax import lax
 from jax.sharding import PartitionSpec as P
+from jax.lax import axis_index, ppermute, psum
 
 EPSILON = 1e-12
 NEGATIVE = -1e30
+
+
+def create_classes(mat, peer_axis, axis_no):
+    y2, u_next = (psum(1, peer_axis), axis_index(peer_axis))
+    latest, back = (mat, 1)
+    while back < y2:
+        pages = []
+        for h in range(y2):
+            pages.append((h, h ^ back))
+        current_block = ppermute(latest, peer_axis, pages)
+        formed = jnp.concatenate([latest, current_block], axis_no)
+        reached = jnp.concatenate([current_block, latest], axis_no)
+        latest = jnp.where(u_next & back == 0, formed, reached)
+        back = 2 * back
+    return latest
+
+
+lay_the_record = functools.partial(create_classes, peer_axis=("row", "col"), axis_no=0)
 
 
 def gather_feats(shard):
@@ -172,7 +192,7 @@
     up_blocks = jnp.transpose(w_up)
     down_blocks = jnp.transpose(w_down)
     whole = (
-        lax.all_gather(qkv_blocks[None], ("row", "col"), axis=0, tiled=True),
+        lay_the_record(qkv_blocks[None]),
         lax.all_gather(w_out[None], ("row", "col"), axis=0, tiled=True),
         lax.all_gather(up_blocks[None], ("row", "col"), axis=0, tiled=True),
         lax.all_gather(down_blocks[None], ("row", "col"), axis=0, tiled=True),

time: 987 us -> 1050 us (1.064)
  blocking collectives: 178 us -> 272 us
  waiting for transfers between devices: 413 us -> 364 us
    all_gather x1, blocking collectives: 13.6 us -> 108 us  [per_device(): lax.all_gather(bias_qv, 'row', axis=0, tiled=True)]
    ppermute x0 -> x4, waiting for transfers between devices: none -> 48 us  [create_classes(): current_block = ppermute(latest, peer_axis, pages)]
    all_gather x1 -> x0, waiting for transfers between devices: 47.3 us -> none  [per_device(): lax.all_gather(qkv_blocks[None], ('row', 'col'), axis=0, tiled=True)]
    all_gather x2, waiting for transfers between devices: 39.1 us -> 14 us  [gather_feats(): return lax.all_gather(shard, 'col', axis=1, tiled=True)]
    all_gather x1, waiting for transfers between devices: 24.4 us -> 0.01 us  [per_device(): lax.all_gather(w_out[None], ('row', 'col'), axis=0, tiled=True)]
    reshape x6 -> x5, local copies, waits for them, and re-layouts: 37.7 us -> 29.1 us  [assemble(): grid = stacked.reshape((row_size, col_size) + shape[1:])]
  transfers between devices with their start and end apart: 17 -> 20, of which waited for: 14 -> 14; matrix products, arithmetic and copies ran while one was open for 10% -> 11% of each run, Pallas kernels for 0% -> 0%
where the time goes in v1:
time: 1050 us; the launch traced here: 1040 us
  waiting for transfers between devices  364 us (35%)
  blocking collectives  272 us (26%)
  matrix products  161 us (15%)
  local copies, waits for them, and re-layouts  135 us (13%)
  other arithmetic  80.5 us (8%)
  between operations  15.6 us (1%)
    all_gather x1, blocking collectives, per_device(): lax.all_gather(bias_qv, 'row', axis=0, tiled=True)  108 us
    reduce_scatter x2, waiting for transfers between devices, forward_reduce(): lax.psum_scatter(partial_rows.astype(jnp.bfloat16), 'col', scatter_dimens...  73.3 us
    all_gather x2, waiting for transfers between devices, back_gather(): return lax.all_gather(shard, 'col', axis=1, tiled=True)  60 us
    reduce_scatter x2, waiting for transfers between devices, backward_reduce(): lax.psum_scatter(partial_rows.astype(jnp.bfloat16), 'col', scatter_dimens...  56.7 us
    ppermute x4, waiting for transfers between devices, create_classes(): current_block = ppermute(latest, peer_axis, pages)  48 us
    dot_general x4, matrix products, against(): lax.dot_general(piece_rows, matrix, (((1,), (1,)), ((), ())), preferred_e...  40.1 us
    psum x1, blocking collectives, per_device(): lax.psum((heads_pad, units_pad, feat_pad), ('dp', 'row', 'col'))  39.6 us
    all_gather x1, waiting for transfers between devices, per_device(): lax.all_gather(down_blocks[None], ('row', 'col'), axis=0, tiled=True)  38.2 us
  transfers between devices with their start and end apart: 20, of which 14 were waited for; matrix products, arithmetic and copies ran while one was open for 11% of the time, Pallas kernels for 0%

profile of v1, /device:TPU:0, one launch (start us, length us, event | category | flops | bytes accessed | tf_op | source)
XLA Modules:
  0.0 1039.3 jit_solution(1490568451127423214)
XLA Ops:
  18.6 14.7 %collective-permute-done.1 = bf16[2,3,192,192]{3,2,1,0:T(8,128)(2,1)S(1)} collective-permute-done((bf16[2,3,192,192]{3,2,1,0:T(8,128)(2,1)S(1)}, bf16[2,3,192,192]{3,2,1,0:T(8,128)(2,1)S(1)}, u32[]{:S(2)}, u32[]{:S(2)}) %collective-permute-start.1) | collective-permute-done | bytes 442400 | tf_op jit(solution)/shard_map/ppermute | solution.py:20
  35.5 32.1 %collective-permute-done.2 = bf16[4,3,192,192]{3,2,1,0:T(8,128)(2,1)} collective-permute-done((bf16[4,3,192,192]{3,2,1,0:T(8,128)(2,1)S(1)}, bf16[4,3,192,192]{3,2,1,0:T(8,128)(2,1)}, u32[]{:S(2)}, u32[]{:S(2)}) %collective-permute-start.2) | collective-permute-done | bytes 884768 | tf_op jit(solution)/shard_map/ppermute | solution.py:20
  72.3 107.9 %all-gather.3 = f32[4,3,128]{2,1,0:T(4,128)S(1)} all-gather(f32[1,3,128]{2,1,0:T(4,128)S(1)} %bitcast.266), channel_id=1, replica_groups=mesh['dp'=2,'row'=4,'col'=4] {'row'}, dimensions={0}, use_global_device_ids=true | all-gather | bytes 7680 | tf_op jit(solution)/shard_map/all_gather | solution.py:211
  180.3 3.8 copy.153
  184.1 4.0 reshape.243
  188.1 6.3 maximum_select_fusion
  194.4 9.7 copy.109
  204.1 7.7 reshape.239
  212.7 7.4 reshape.276
  220.1 3.5 fusion.60
  224.5 51.6 %while.26 = (s32[]{:T(128)}, bf16[2,1044,3,64]{1,3,2,0:T(8,128)(2,1)S(1)}, f32[2,3,1044]{2,1,0:T(4,128)}, bf16[2,1044,3,64]{1,3,2,0:T(8,128)(2,1)S(1)}, s32[2,10...) while((s32[]{:T(128)}, ...), condition=%wide.region_3.4_spmd, body=%wide.region_0.3_spmd.sunk | while | flops 864516608 | bytes 43690424 | solution.py:228
  227.0 8.0 fusion.151
  235.0 7.1 fusion.152
  242.1 7.8 fusion.153
  252.5 8.0 fusion.151
  260.5 7.1 fusion.152
  267.6 7.8 fusion.153
  281.1 4.1 convolution_convert_fusion.3
  286.7 36.1 %reduce-scatter.9.cloned.1.call-done = bf16[2088,192]{0,1:T(8,128)(2,1)} async-done(((bf16[2088,768]{0,1:T(8,128)(2,1)}), bf16[2088,192]{0,1:T(8,128)(2,1)}) %reduce-scatter.9.cloned.1.call-update) | async-done | bytes 801808 | tf_op jit(solution)/shard_map/reduce_scatter | solution.py:40
  324.4 10.3 all-reduce.5
  337.4 13.3 %all-gather.4 = f32[4,1,768]{2,1,0:T(1,128)S(1)} all-gather(f32[1,1,768]{2,1,0:T(1,128)S(1)} %reshape.263), channel_id=1, replica_groups=mesh['dp'=2,'row'=4,'col'=4] {'row'}, dimensions={0}, use_global_device_ids=true | all-gather | bytes 15360 | tf_op jit(solution)/shard_map/all_gather | solution.py:212
  350.8 27.6 %all-gather.23.cloned.1.call-done = bf16[12288,192]{0,1:T(8,128)(2,1)} async-done(((bf16[768,192]{0,1:T(8,128)(2,1)}), bf16[12288,192]{0,1:T(8,128)(2,1)}) %all-gather.23.cloned.1.call-update) | async-done | bytes 4718608 | tf_op jit(solution)/shard_map/all_gather | solution.py:197
  378.3 8.3 reshape.244
  386.6 4.3 copy.112
  394.1 38.2 %all-gather.25.cloned.1.call-done = bf16[12288,192]{0,1:T(8,128)(2,1)} async-done(((bf16[768,192]{0,1:T(8,128)(2,1)}), bf16[12288,192]{0,1:T(8,128)(2,1)}) %all-gather.25.cloned.1.call-update) | async-done | bytes 4718608 | tf_op jit(solution)/shard_map/all_gather | solution.py:198
  432.2 8.3 reshape.246
  440.5 4.5 copy.113
  448.2 14.0 %all-gather.15.cloned.1.call-done = bf16[2088,768]{0,1:T(8,128)(2,1)} async-done(((bf16[2088,192]{0,1:T(8,128)(2,1)}), bf16[2088,768]{0,1:T(8,128)(2,1)}) %all-gather.15.cloned.1.call-update) | async-done | bytes 3207184 | tf_op jit(solution)/shard_map/all_gather | solution.py:32
  462.2 20.0 %multiply_convert_fusion.1 = (bf16[2088,768]{1,0:T(8,128)(2,1)S(1)}, f32[2088,768]{1,0:T(8,128)}, f32[2088,768]{1,0:T(8,128)}) fusion(f32[768]{0:T(1024)S(1)} %dynamic_slice.67, bf16[2088,768]{0,1:T(8,128)(2,1)} %all-gather.15.cloned.1.call-done, bf16[3072,768]{0,1:T(8,128)(2,1)} %bitcast.238, s32[]{:T(128)S(6)} %select_n.83), kind=kOutput, calls=%fused_computation.65 | convolution fusion | flops 2568941568 | bytes 20560900 | tf_op jit(solution)/shard_map/dot_general | solution.py:52
  483.8 6.0 convolution_convert_fusion.2
  492.0 37.2 %reduce-scatter.11.cloned.1.call-done = bf16[2088,192]{0,1:T(8,128)(2,1)} async-done(((bf16[2088,768]{0,1:T(8,128)(2,1)}), bf16[2088,192]{0,1:T(8,128)(2,1)}) %reduce-scatter.11.cloned.1.call-update) | async-done | bytes 801808 | tf_op jit(solution)/shard_map/reduce_scatter | solution.py:40
  531.4 10.6 %all-reduce.4 = (f32[2088]{0:T(1024)S(1)}, f32[2088]{0:T(1024)S(1)}) all-reduce(f32[2088]{0:T(1024)S(1)} %get-tuple-element.161, f32[2088]{0:T(1024)S(1)} %get-tuple-element.160), channel_id=1, replica_groups=mesh['dp'=2,'row'=4,'col'=4] {'col'}, use_global_device_ids=true, to_apply=%region_13.14 | all-reduce | flops 4176 | bytes 33408 | tf_op jit(solution)/shard_map/psum | solution.py:76
  543.6 3.5 reshape.248
  553.0 4.6 pad.4.clone
  563.3 10.3 all-reduce.3
  576.9 29.9 %all-gather.17.cloned.1.call-done = bf16[2088,768]{0,1:T(8,128)(2,1)} async-done(((bf16[2088,192]{0,1:T(8,128)(2,1)}), bf16[2088,768]{0,1:T(8,128)(2,1)}) %all-gather.17.cloned.1.call-update) | async-done | bytes 3207184 | tf_op jit(solution)/shard_map/all_gather | solution.py:36
  606.9 10.5 %add_convert_fusion = bf16[2088,768]{1,0:T(8,128)(2,1)S(1)} fusion(f32[2088,768]{1,0:T(8,128)} %get-tuple-element.216, f32[2088,768]{1,0:T(8,128)} %get-tuple-element.241, bf16[2088,768]{0,1:T(8,128)(2,1)} %all-gather.17.cloned.1.call-done, bf16[3072,768]{0,1:T(8,128)(2,1)} %bitcast.241, s32[]{:T(128)S(6)} %select_n.83), kind=kOutput, calls=%fused_computation.64 | convolution fusion | flops 2485555200 | bytes 20557828 | tf_op jit(solution)/shard_map/dot_general | solution.py:52
  619.0 5.9 convolution_convert_fusion.1
  625.0 39.2 %reduce-scatter.13.cloned.1.call-done = bf16[2088,192]{0,1:T(8,128)(2,1)} async-done(((bf16[2088,768]{0,1:T(8,128)(2,1)}), bf16[2088,192]{0,1:T(8,128)(2,1)}) %reduce-scatter.13.cloned.1.call-update) | async-done | bytes 801808 | tf_op jit(solution)/shard_map/reduce_scatter | solution.py:46
  664.3 5.1 multiply_reduce_fusion.3
  669.3 10.3 all-reduce.2
  682.9 30.1 %all-gather.19.cloned.1.call-done = bf16[2088,768]{0,1:T(8,128)(2,1)} async-done(((bf16[2088,192]{0,1:T(8,128)(2,1)}), bf16[2088,768]{0,1:T(8,128)(2,1)}) %all-gather.19.cloned.1.call-update) | async-done | bytes 3207184 | tf_op jit(solution)/shard_map/all_gather | solution.py:36
  713.1 3.7 convolution_convert_fusion.4
  723.6 68.2 %while.27 = (s32[]{:T(128)}, bf16[2,1044,3,64]{1,3,2,0:T(8,128)(2,1)}, bf16[2,1044,3,64]{1,3,2,0:T(8,128)(2,1)}, bf16[2,1044,3,64]{1,3,2,0:T(8,128)(2,1)}, bf16[...) while((s32[]{:T(128)}, ...), condition=%wide.region_26.27_spmd, body=%wide.region_24.26_spmd.sunk | while | flops 2124194560 | bytes 151329200 | solution.py:282
  724.5 3.4 fusion.162
  728.0 8.2 multiply_reduce_fusion.10
  736.2 8.6 multiply_convert_fusion.3
  744.8 8.3 fusion.165
  758.5 3.4 fusion.162
  762.0 8.2 multiply_reduce_fusion.10
  770.2 8.6 multiply_convert_fusion.3
  778.8 8.3 fusion.165
  799.4 5.0 fusion.72
  805.4 22.5 %all_to_all.75 = bf16[3,768,192]{2,0,1:T(4,128)(2,1)S(1)} all-to-all(bf16[3,768,192]{2,0,1:T(4,128)(2,1)S(1)} %copy.122), channel_id=1, replica_groups=mesh['dp'=2,'row'=4,'col'=4] {'col'}, dimensions={1} | all-to-all | bytes 1769472 | tf_op jit(solution)/shard_map/all_to_all | solution.py:296
  830.3 4.8 convolution_convert_fusion.5
  835.1 18.5 %all_to_all.76 = bf16[768,4,192]{0,2,1:T(8,128)(2,1)S(1)} all-to-all(bf16[768,4,192]{0,2,1:T(8,128)(2,1)S(1)} %bitcast.250), channel_id=1, replica_groups=mesh['dp'=2,'row'=4,'col'=4] {'col'}, dimensions={1} | all-to-all | bytes 2359296 | tf_op jit(solution)/shard_map/all_to_all | solution.py:305
  854.9 4.9 convolution_convert_fusion.6
  859.8 18.4 %all_to_all.77 = bf16[768,4,192]{0,2,1:T(8,128)(2,1)S(1)} all-to-all(bf16[768,4,192]{0,2,1:T(8,128)(2,1)S(1)} %bitcast.251), channel_id=1, replica_groups=mesh['dp'=2,'row'=4,'col'=4] {'col'}, dimensions={1} | all-to-all | bytes 2359296 | tf_op jit(solution)/shard_map/all_to_all | solution.py:302
  883.4 10.6 %all_to_all.78 = bf16[192,4,192]{2,0,1:T(8,128)(2,1)} all-to-all(bf16[192,4,192]{2,0,1:T(8,128)(2,1)S(1)} %copy.125), channel_id=1, replica_groups=mesh['dp'=2,'row'=4,'col'=4] {'col'}, dimensions={1} | all-to-all | bytes 589824 | tf_op jit(solution)/shard_map/all_to_all | solution.py:299
  896.1 22.9 %reduce-scatter.21.cloned.1.call-done = bf16[768,192]{0,1:T(8,128)(2,1)} async-done(((bf16[3072,192]{0,1:T(8,128)(2,1)}), bf16[768,192]{0,1:T(8,128)(2,1)}) %reduce-scatter.21.cloned.1.call-update) | async-done | bytes 294928 | tf_op jit(solution)/shard_map/reduce_scatter | solution.py:316
  919.0 21.6 %reduce-scatter.19.cloned.1.call-done = bf16[192,192]{1,0:T(8,128)(2,1)} async-done(((bf16[768,192]{1,0:T(8,128)(2,1)}), bf16[192,192]{1,0:T(8,128)(2,1)}) %reduce-scatter.19.cloned.1.call-update) | async-done | bytes 73744 | tf_op jit(solution)/shard_map/reduce_scatter | solution.py:313
  940.6 5.8 convolution_convert_fusion
  956.1 39.6 %all-reduce.1 = (f32[12,128]{1,0:T(8,128)S(1)}, f32[6,768]{1,0:T(8,128)S(1)}, f32[3072]{0:T(1024)S(1)}) all-reduce(f32[12,128]{1,0:T(8,128)S(1)} %dynamic_update_slice.26, f32[6,768]{1,0:T(8,128)S(1)} %dynamic_update_slice.27, f32[3072]{0:T(1024)S(1)} %dynamic_update_slice.28), channel_id=1, replica_groups=mesh['dp'=2,'row'=4,'col'=4] {'dp','row','col'}, use_global_device_ids=true, to_apply=%region_30.31 | all-reduce | flops 9216 | bytes 73728 | tf_op jit(solution)/shard_map/psum | solution.py:348
  1004.7 17.5 %reduce-scatter.15.cloned.1.call-done = bf16[2088,192]{0,1:T(8,128)(2,1)} async-done(((bf16[2088,768]{0,1:T(8,128)(2,1)}), bf16[2088,192]{0,1:T(8,128)(2,1)}) %reduce-scatter.15.cloned.1.call-update) | async-done | bytes 801808 | tf_op jit(solution)/shard_map/reduce_scatter | solution.py:46
  (292 shorter events, 135.5 us)
Async XLA Ops:
  7.2 173.2 %all-gather.21.cloned.1.call-start = ((), (), s32[]{:S(2)}) async-start(), calls=%async_computation.24 | async-start | bytes 1671168 | tf_op jit(solution)/shard_map/all_gather | solution.py:196
  7.9 204.8 %all-gather.13.cloned.1.call-start = ((), (), s32[]{:S(2)}) async-start(), calls=%async_computation.12 | async-start | bytes 4177920 | tf_op jit(solution)/shard_map/all_gather | solution.py:32
  13.3 309.4 %reduce-scatter.9.cloned.1.call-start = ((), (), s32[]{:S(2)}) async-start(), calls=%async_computation.13 | async-start | bytes 4177920 | tf_op jit(solution)/shard_map/reduce_scatter | solution.py:40
  13.7 1.8 collective-permute-start
  15.6 17.6 %collective-permute-start.1 = (bf16[2,3,192,192]{3,2,1,0:T(8,128)(2,1)S(1)}, bf16[2,3,192,192]{3,2,1,0:T(8,128)(2,1)S(1)}, u32[]{:S(2)}, u32[]{:S(2)}) collective-permute-start(bf16[2,3,192,192]{3,2,1,0:T(8,128)(2,1)S(1)} %maximum_select_fusion.3), channel_id=1, source_target_pairs={{0,2},{1,3},{2,0},{3,1},{4,6},{5,7},{6,4},{7,5},{8,10},{9,11},{10,... | collective-permute-start | bytes 1327112 | tf_op jit(solution)/shard_map/ppermute | solution.py:20
  18.6 53.8 %copy-start.50 = (f32[3,128]{1,0:T(4,128)S(1)}, f32[3,128]{1,0:T(4,128)}, u32[]{:S(2)}) copy-start(f32[3,128]{1,0:T(4,128)} %param.27) | copy-start | bytes 4612
  33.7 34.0 %collective-permute-start.2 = (bf16[4,3,192,192]{3,2,1,0:T(8,128)(2,1)S(1)}, bf16[4,3,192,192]{3,2,1,0:T(8,128)(2,1)}, u32[]{:S(2)}, u32[]{:S(2)}) collective-permute-start(bf16[4,3,192,192]{3,2,1,0:T(8,128)(2,1)S(1)} %maximum_select_fusion.2), channel_id=1, source_target_pairs={{0,4},{1,5},{2,6},{3,7},{4,0},{5,1},{6,2},{7,3},{8,12},{9,13},{10,... | collective-permute-start | bytes 2654216 | tf_op jit(solution)/shard_map/ppermute | solution.py:20
  69.8 118.3 %collective-permute-start.3 = (bf16[8,3,192,192]{3,2,1,0:T(8,128)(2,1)S(1)}, bf16[8,3,192,192]{3,2,1,0:T(8,128)(2,1)}, u32[]{:S(2)}, u32[]{:S(2)}) collective-permute-start(bf16[8,3,192,192]{3,2,1,0:T(8,128)(2,1)S(1)} %maximum_select_fusion.1), channel_id=1, source_target_pairs={{0,8},{1,9},{2,10},{3,11},{4,12},{5,13},{6,14},{7,15},{8,0},{9,1},... | collective-permute-start | bytes 5308424 | tf_op jit(solution)/shard_map/ppermute | solution.py:20
  242.1 7.8 copy-start.30
  242.1 8.4 copy-start.34
  267.6 7.8 copy-start.30
  267.6 8.4 copy-start.34
  276.1 5.1 copy-start.3
  276.1 9.1 copy-start.5
  285.2 37.5 %copy-start.1 = (bf16[2088,192]{0,1:T(8,128)(2,1)S(1)}, bf16[2088,192]{0,1:T(8,128)(2,1)}, u32[]{:S(2)}) copy-start(bf16[2088,192]{0,1:T(8,128)(2,1)} %reshape.238) | copy-start | bytes 2405380
  285.2 37.5 %copy-start.39 = (f32[192]{0:T(256)S(1)}, f32[192]{0:T(256)}, u32[]{:S(2)}) copy-start(f32[192]{0:T(256)} %param.29) | copy-start | bytes 2308
  285.2 49.5 %copy-start.42 = (f32[192]{0:T(256)S(1)}, f32[192]{0:T(256)}, u32[]{:S(2)}) copy-start(f32[192]{0:T(256)} %param.30) | copy-start | bytes 2308
  285.2 49.5 %copy-start.44 = (f32[192]{0:T(256)S(1)}, f32[192]{0:T(256)}, u32[]{:S(2)}) copy-start(f32[192]{0:T(256)} %param.31) | copy-start | bytes 2308
  285.3 52.1 %copy-start.48 = (f32[768]{0:T(1024)S(1)}, f32[768]{0:T(1024)}, u32[]{:S(2)}) copy-start(f32[768]{0:T(1024)} %param.33) | copy-start | bytes 9220
  285.3 93.1 %all-gather.23.cloned.1.call-start = ((), (), s32[]{:S(2)}) async-start(), calls=%async_computation.25 | async-start | bytes 5013504 | tf_op jit(solution)/shard_map/all_gather | solution.py:197
  285.9 146.4 %all-gather.25.cloned.1.call-start = ((), (), s32[]{:S(2)}) async-start(), calls=%async_computation.26 | async-start | bytes 5013504 | tf_op jit(solution)/shard_map/all_gather | solution.py:198
  286.4 175.8 %all-gather.15.cloned.1.call-start = ((), (), s32[]{:S(2)}) async-start(), calls=%async_computation.14 | async-start | bytes 4177920 | tf_op jit(solution)/shard_map/all_gather | solution.py:32
  334.6 344.9 %copy-start.25 = (f32[2088]{0:T(1024)}, f32[2088]{0:T(1024)S(1)}, u32[]{:S(2)}) copy-start(f32[2088]{0:T(1024)S(1)} %get-tuple-element.235) | copy-start | bytes 25060
  334.7 344.9 %copy-start.27 = (f32[2088]{0:T(1024)}, f32[2088]{0:T(1024)S(1)}, u32[]{:S(2)}) copy-start(f32[2088]{0:T(1024)S(1)} %get-tuple-element.236) | copy-start | bytes 25060
  337.4 191.8 %reduce-scatter.11.cloned.1.call-start = ((), (), s32[]{:S(2)}) async-start(), calls=%async_computation.15 | async-start | bytes 4177920 | tf_op jit(solution)/shard_map/reduce_scatter | solution.py:40
  489.8 39.3 %copy-start.8 = (bf16[2088,192]{0,1:T(8,128)(2,1)S(1)}, bf16[2088,192]{0,1:T(8,128)(2,1)}, u32[]{:S(2)}) copy-start(bf16[2088,192]{0,1:T(8,128)(2,1)} %reduce-scatter.9.cloned.1.call-done) | copy-start | bytes 2405380
  489.8 39.3 %copy-start.51 = (f32[192]{0:T(256)S(1)}, f32[192]{0:T(256)}, u32[]{:S(2)}) copy-start(f32[192]{0:T(256)} %param.35) | copy-start | bytes 2308
  489.8 52.2 %copy-start.41 = (f32[192]{0:T(256)S(1)}, f32[192]{0:T(256)}, u32[]{:S(2)}) copy-start(f32[192]{0:T(256)} %param.36) | copy-start | bytes 2308
  489.8 52.2 %copy-start.52 = (f32[192]{0:T(256)S(1)}, f32[192]{0:T(256)}, u32[]{:S(2)}) copy-start(f32[192]{0:T(256)} %param.37) | copy-start | bytes 2308
  489.9 117.0 %all-gather.17.cloned.1.call-start = ((), (), s32[]{:S(2)}) async-start(), calls=%async_computation.16 | async-start | bytes 4177920 | tf_op jit(solution)/shard_map/all_gather | solution.py:36
  576.4 87.8 %reduce-scatter.13.cloned.1.call-start = ((), (), s32[]{:S(2)}) async-start(), calls=%async_computation.17 | async-start | bytes 4177920 | tf_op jit(solution)/shard_map/reduce_scatter | solution.py:46
  625.0 88.1 %all-gather.19.cloned.1.call-start = ((), (), s32[]{:S(2)}) async-start(), calls=%async_computation.18 | async-start | bytes 4177920 | tf_op jit(solution)/shard_map/all_gather | solution.py:36
  679.6 37.2 %copy-start.35 = (f32[2088]{0:T(1024)}, f32[2088]{0:T(1024)S(1)}, u32[]{:S(2)}) copy-start(f32[2088]{0:T(1024)S(1)} %broadcast_multiply_fusion) | copy-start | bytes 25060
  679.6 37.2 %copy-start.37 = (f32[2088]{0:T(1024)}, f32[2088]{0:T(1024)S(1)}, u32[]{:S(2)}) copy-start(f32[2088]{0:T(1024)S(1)} %broadcast_multiply_fusion.1) | copy-start | bytes 25060
  682.7 211.4 %reduce-scatter.17.cloned.1.call-start = ((), (), s32[]{:S(2)}) async-start(), calls=%async_computation.20 | async-start | bytes 1474560 | tf_op jit(solution)/shard_map/reduce_scatter | solution.py:310
  716.8 6.9 copy-start.4
  716.8 6.9 copy-start.6
  716.8 6.9 copy-start.32
  736.2 8.6 copy-start.7
  744.8 8.3 copy-start
  744.8 8.3 copy-start.17
  770.2 8.6 copy-start.7
  778.8 8.3 copy-start
  778.8 8.3 copy-start.17
  829.1 67.0 %reduce-scatter.23.cloned.1.call-start = ((), (), s32[]{:S(2)}) async-start(), calls=%async_computation.23 | async-start | bytes 1474560 | tf_op jit(solution)/shard_map/reduce_scatter | solution.py:319
  835.1 19.8 %copy-start.22 = (bf16[2088,768]{1,0:T(8,128)(2,1)S(1)}, bf16[2088,768]{1,0:T(8,128)(2,1)}, u32[]{:S(2)}) copy-start(bf16[2088,768]{1,0:T(8,128)(2,1)} %copy-done.21) | copy-start | bytes 9621508
  854.8 64.2 %reduce-scatter.21.cloned.1.call-start = ((), (), s32[]{:S(2)}) async-start(), calls=%async_computation.22 | async-start | bytes 1474560 | tf_op jit(solution)/shard_map/reduce_scatter | solution.py:316
  859.8 20.1 %copy-start.13 = (bf16[2088,192]{0,1:T(8,128)(2,1)S(1)}, bf16[2088,192]{0,1:T(8,128)(2,1)}, u32[]{:S(2)}) copy-start(bf16[2088,192]{0,1:T(8,128)(2,1)} %copy-done.12) | copy-start | bytes 2405380
  879.4 61.2 %reduce-scatter.19.cloned.1.call-start = ((), (), s32[]{:S(2)}) async-start(), calls=%async_computation.21 | async-start | bytes 491520 | tf_op jit(solution)/shard_map/reduce_scatter | solution.py:313
  883.0 57.7 %copy-start.15 = (bf16[2088,576]{0,1:T(8,128)(2,1)S(1)}, bf16[2088,576]{0,1:T(8,128)(2,1)}, u32[]{:S(2)}) copy-start(bf16[2088,576]{0,1:T(8,128)(2,1)} %reshape.251) | copy-start | bytes 7216132
  894.0 103.6 %all-reduce.9.cloned.1.call-start = ((), (), s32[]{:S(2)}) async-start(), calls=%async_computation.27 | async-start | bytes 1966080 | tf_op jit(solution)/shard_map/psum | solution.py:324
  940.6 81.6 %reduce-scatter.15.cloned.1.call-start = ((), (), s32[]{:S(2)}) async-start(), calls=%async_computation.19 | async-start | bytes 4177920 | tf_op jit(solution)/shard_map/reduce_scatter | solution.py:46
  948.2 4.8 copy-start.46
  948.2 4.9 copy-start.47
  948.2 4.9 copy-start.49
  951.3 70.9 %copy-start.2 = (bf16[2088,192]{0,1:T(8,128)(2,1)S(1)}, bf16[2088,192]{0,1:T(8,128)(2,1)}, u32[]{:S(2)}) copy-start(bf16[2088,192]{0,1:T(8,128)(2,1)} %reshape.238) | copy-start | bytes 2405380
  951.3 70.9 %copy-start.9 = (bf16[2088,192]{0,1:T(8,128)(2,1)S(1)}, bf16[2088,192]{0,1:T(8,128)(2,1)}, u32[]{:S(2)}) copy-start(bf16[2088,192]{0,1:T(8,128)(2,1)} %reduce-scatter.9.cloned.1.call-done) | copy-start | bytes 2405380
  951.3 70.9 %copy-start.11 = (f32[2088,192]{0,1:T(8,128)S(1)}, f32[2088,192]{0,1:T(8,128)}, u32[]{:S(2)}) copy-start(f32[2088,192]{0,1:T(8,128)} %get-tuple-element.213) | copy-start | bytes 4810756
  951.3 70.9 %copy-start.26 = (f32[2088]{0:T(1024)S(1)}, f32[2088]{0:T(1024)}, u32[]{:S(2)}) copy-start(f32[2088]{0:T(1024)} %copy-done.25) | copy-start | bytes 25060
  951.3 70.9 %copy-start.28 = (f32[2088]{0:T(1024)S(1)}, f32[2088]{0:T(1024)}, u32[]{:S(2)}) copy-start(f32[2088]{0:T(1024)} %copy-done.27) | copy-start | bytes 25060
  951.4 70.9 %copy-start.36 = (f32[2088]{0:T(1024)S(1)}, f32[2088]{0:T(1024)}, u32[]{:S(2)}) copy-start(f32[2088]{0:T(1024)} %copy-done.35) | copy-start | bytes 25060
  951.4 70.9 %copy-start.38 = (f32[2088]{0:T(1024)S(1)}, f32[2088]{0:T(1024)}, u32[]{:S(2)}) copy-start(f32[2088]{0:T(1024)} %copy-done.37) | copy-start | bytes 25060
  951.4 70.9 %copy-start.40 = (f32[192]{0:T(256)S(1)}, f32[192]{0:T(256)}, u32[]{:S(2)}) copy-start(f32[192]{0:T(256)} %param.29) | copy-start | bytes 2308
  951.4 70.9 %copy-start.43 = (f32[192]{0:T(256)S(1)}, f32[192]{0:T(256)}, u32[]{:S(2)}) copy-start(f32[192]{0:T(256)} %param.30) | copy-start | bytes 2308
  (21 other events, 40.2 us)
Sparse Core Ops, SparseCore 0:
  10.3 44.6 all-gather.20
  56.5 29.2 all-gather.12
  285.4 37.2 reduce-scatter.8
  324.8 53.5 all-gather.22
  380.4 51.7 all-gather.24
  434.2 27.9 all-gather.14
  490.0 39.1 reduce-scatter.10
  576.6 30.2 all-gather.16
  625.1 39.1 reduce-scatter.12
  682.8 30.1 all-gather.18
  829.2 29.3 reduce-scatter.16
  860.8 27.9 reduce-scatter.22
  891.0 27.9 reduce-scatter.20
  921.1 19.3 reduce-scatter.18
  943.5 37.1 all-reduce.8
  983.1 39.0 reduce-scatter.14
